TPU v7x, 32 devices: a whole 2x2x4 slice. The times are simulated.
32 devices in a mesh: seq: 16 (over z, y, core), chan: 2 (over x).
Axes of the slice: x: 2, y: 2, z: 4, core: 2. Of those that a mesh axis runs over, the one named last changes fastest.
Arguments:
- inputs: bfloat16 [512, 512, 512], P('chan', 'seq'), may hold values from -6 to 6
- gate_in: bfloat16 [512, 512, 512], P('chan', 'seq'), may hold values from -6 to 6
- gate_out: bfloat16 [512, 512, 512], P('seq', 'chan'), may hold values from -6 to 6
- cotangent: bfloat16 [512, 512, 512], P('seq', 'chan'), may hold values from -6 to 6
- mix_one: bfloat16 [512, 512, 512], P('seq', 'chan'), may hold values from -6 to 6
- second_mixing_blocks: bfloat16 [512, 512, 512], P('seq', 'chan'), may hold values from -6 to 6
Outputs:
- grad_input: bfloat16 [512, 512, 512], P('chan', 'seq')
- grad_gate_out: bfloat16 [512, 512, 512], P('seq', 'chan')
- grad_mix_one: bfloat16 [512, 512, 512], P('seq', 'chan')
- grad_mix_two: bfloat16 [512, 512, 512], P('seq', 'chan')
All inputs are finite; a program needn't handle non-finite values.
Results may differ from a plain program's by a relative error of at most 0.0095.
Values may be sent and summed in bfloat16 or wider, within the bound.
A program may use at most 256 MiB of HBM per device.

v0:
```python
import math

import jax
import jax.numpy as jnp
from jax import lax
from jax.sharding import PartitionSpec as P


def shards(inputs, gate_in, gate_out, cotangent, mix_one, second_mixing_blocks):
    chan_count = lax.axis_size("chan")
    first_scale = 1.0 / math.sqrt(mix_one.shape[2])
    scale_two = 1.0 / math.sqrt(second_mixing_blocks.shape[2])
    gated = (inputs.astype(jnp.float32) * gate_in.astype(jnp.float32)).astype(jnp.bfloat16)
    grad_second = (cotangent.astype(jnp.float32) * gate_out.astype(jnp.float32)).astype(
        jnp.bfloat16
    )
    gated_all = lax.all_gather(gated, "chan", axis=0, tiled=True)
    full_one, full_two = (
        lax.all_gather(mix_one, "chan", axis=1, tiled=True),
        lax.all_gather(second_mixing_blocks, "chan", axis=1, tiled=True),
    )
    first = (
        jnp.einsum("roi,dri->odr", full_one, gated, preferred_element_type=jnp.float32)
        * first_scale
    ).astype(jnp.bfloat16)
    first_cols = lax.all_to_all(first, "seq", split_axis=0, concat_axis=2, tiled=True)
    first_all = lax.all_gather(first_cols, "chan", axis=1, tiled=True)
    second = (
        jnp.einsum("coi,cdi->cdo", full_two, first_cols, preferred_element_type=jnp.float32)
        * scale_two
    ).astype(jnp.bfloat16)
    grad_gate_out = (cotangent.astype(jnp.float32) * second.astype(jnp.float32)).astype(
        jnp.bfloat16
    )
    grad_first_cols = (
        jnp.einsum("coi,cdo->cdi", full_two, grad_second, preferred_element_type=jnp.float32)
        * scale_two
    ).astype(jnp.bfloat16)
    grad_second_rows = lax.all_to_all(grad_second, "chan", split_axis=2, concat_axis=1, tiled=True)
    grad_mix_two = (
        jnp.einsum("cdo,cdi->coi", grad_second_rows, first_all, preferred_element_type=jnp.float32)
        * scale_two
    ).astype(jnp.bfloat16)
    grad_first = lax.all_to_all(grad_first_cols, "seq", split_axis=2, concat_axis=0, tiled=True)
    grad_part = lax.all_to_all(grad_first, "chan", split_axis=0, concat_axis=1, tiled=True)
    grad_mix_one = (
        jnp.einsum("odr,dri->roi", grad_part, gated_all, preferred_element_type=jnp.float32)
        * first_scale
    ).astype(jnp.bfloat16)
    rows_here, columns, _ = full_one.shape
    group_weight = full_one.reshape(rows_here, chan_count, columns // chan_count, columns)
    group_grad = grad_first.reshape(
        chan_count, columns // chan_count, grad_first.shape[1], rows_here
    )
    summand_terms = (
        jnp.einsum("rgoi,godr->gdri", group_weight, group_grad, preferred_element_type=jnp.float32)
        * first_scale
    ).astype(jnp.bfloat16)
    grad_gated = jnp.sum(summand_terms.astype(jnp.float32), axis=0).astype(jnp.bfloat16)
    grad_input = (grad_gated.astype(jnp.float32) * gate_in.astype(jnp.float32)).astype(jnp.bfloat16)
    return (grad_input, grad_gate_out, grad_mix_one, grad_mix_two)


def solution(mesh):
    return jax.shard_map(
        shards,
        mesh=mesh,
        in_specs=(
            P("chan", "seq", None),
            P("chan", "seq", None),
            P("seq", "chan", None),
            P("seq", "chan", None),
            P("seq", "chan", None),
            P("seq", "chan", None),
        ),
        out_specs=(
            P("chan", "seq", None),
            P("seq", "chan", None),
            P("seq", "chan", None),
            P("seq", "chan", None),
        ),
        check_vma=False,
    )
```

profile of v0, /device:TPU:0, one launch (start us, length us, event | category | flops | bytes accessed | tf_op | source)
XLA Modules:
  0.0 1185.0 jit_solution(13639298940770544008)
XLA Ops:
  7.2 0.0 all-gather.5.cloned.1.call-start
  7.2 0.7 all-gather.5.cloned.1.call-update
  7.9 0.0 all-gather.7.cloned.1.call-start
  7.9 0.7 all-gather.7.cloned.1.call-update
  8.6 0.0 all-gather.9.cloned.1.call-start
  8.7 9.9 fusion
  18.6 192.5 %all-gather.5.cloned.1.call-done = bf16[32,512,512]{2,1,0:T(8,128)(2,1)} async-done(((bf16[32,256,512]{2,1,0:T(8,128)(2,1)}), bf16[32,512,512]{2,1,0:T(8,128)(2,1)}) %all-gather.5.cloned.1.call-update) | async-done | bytes 16777232 | tf_op jit(solution)/shard_map/all_gather | solution.py:20
  211.1 15.1 %multiply_convert_fusion.5 = bf16[32,256,512]{2,1,0:T(8,128)(2,1)} fusion(bf16[32,256,512]{2,1,0:T(8,128)(2,1)} %fusion, bf16[32,512,512]{2,1,0:T(8,128)(2,1)} %all-gather.5.cloned.1.call-done), kind=kOutput, calls=%fused_computation.14 | convolution fusion | flops 4303355904 | bytes 33554432 | tf_op jit(solution)/shard_map/coi,cdo->cdi/dot_general | solution.py:36
  226.2 15.2 %copy.29 = bf16[32,256,512]{1,0,2:T(8,128)(2,1)} copy(bf16[32,256,512]{2,1,0:T(8,128)(2,1)} %multiply_convert_fusion.5) | data formatting | bytes 16777216 | tf_op jit(solution)/shard_map/convert_element_type | solution.py:38
  241.3 188.2 %all_to_all.72 = bf16[32,256,512]{1,0,2:T(8,128)(2,1)} all-to-all(bf16[32,256,512]{1,0,2:T(8,128)(2,1)} %copy.29), channel_id=1, replica_groups=mesh['seq'=16,'chan'=2] {'seq'}, dimensions={2} | all-to-all | bytes 16777216 | tf_op jit(solution)/shard_map/all_to_all | solution.py:44
  429.6 12.5 %copy.31 = bf16[16,32,256,32]{2,3,1,0:T(8,128)(2,1)} copy(bf16[16,32,256,32]{2,1,3,0:T(8,128)(2,1)} %bitcast.42) | data formatting | bytes 16777216 | tf_op jit(solution)/shard_map/all_to_all | solution.py:44
  442.1 26.1 %fusion.7 = bf16[32,256,512]{2,1,0:T(8,128)(2,1)} fusion(bf16[32,2,256,512]{3,2,1,0:T(8,128)(2,1)} %bitcast.45, bf16[2,256,256,32]{2,3,1,0:T(8,128)(2,1)} %bitcast.39), kind=kOutput, calls=%fused_computation.18 | convolution fusion | flops 4315938816 | bytes 33554432 | tf_op jit(solution)/shard_map/rgoi,godr->gdri/dot_general | solution.py:56
  468.1 18.1 %fusion.3 = (bf16[256,32,512]{2,0,1:T(8,128)(2,1)}, bf16[256,32,512]{2,0,1:T(8,128)(2,1)}) fusion(bf16[256,32,512]{2,1,0:T(8,128)(2,1)} %param.6, bf16[256,32,512]{2,1,0:T(8,128)(2,1)} %param.7, bf16[32,256,512]{2,1,0:T(8,128)(2,1)} %fusion.7), kind=kLoop, calls=%fused_computation.8 | loop fusion | flops 29360128 | bytes 41943040 | tf_op jit(solution)/shard_map/convert_element_type | solution.py:13
  486.3 0.0 all-gather.9.cloned.1.call-update
  486.3 0.0 all-gather.11.cloned.1.call-start
  486.4 16.1 %fusion.6 = bf16[512,256,32]{0,1,2:T(8,128)(2,1)} fusion(bf16[256,32,512]{2,0,1:T(8,128)(2,1)} %get-tuple-element.16, bf16[32,512,512]{2,1,0:T(8,128)(2,1)} %all-gather.7.cloned.1.call-done), kind=kOutput, calls=%fused_computation.17 | convolution fusion | flops 4303355904 | bytes 33554432 | tf_op jit(solution)/shard_map/roi,dri->odr/dot_general | solution.py:23
  502.5 15.2 %copy.36 = bf16[512,256,32]{1,2,0:T(8,128)(2,1)} copy(bf16[512,256,32]{0,1,2:T(8,128)(2,1)} %fusion.6) | data formatting | bytes 16777216 | tf_op jit(solution)/shard_map/convert_element_type | solution.py:25
  517.6 187.8 %all_to_all.73 = bf16[512,256,32]{1,2,0:T(8,128)(2,1)} all-to-all(bf16[512,256,32]{1,2,0:T(8,128)(2,1)} %copy.36), channel_id=1, replica_groups=mesh['seq'=16,'chan'=2] {'seq'}, dimensions={0} | all-to-all | bytes 16777216 | tf_op jit(solution)/shard_map/all_to_all | solution.py:26
  705.4 8.0 copy.37
  713.4 12.0 %copy.43 = bf16[32,256,512]{2,1,0:T(8,128)(2,1)} copy(bf16[32,256,512]{1,2,0:T(8,128)(2,1)} %bitcast.37) | data formatting | bytes 16777216 | tf_op jit(solution)/shard_map/all_to_all | solution.py:26
  725.4 15.3 %copy.41 = bf16[32,256,512]{1,0,2:T(8,128)(2,1)} copy(bf16[32,256,512]{2,1,0:T(8,128)(2,1)} %fusion) | data formatting | bytes 16777216 | tf_op jit(solution)/shard_map/convert_element_type | solution.py:14
  740.7 195.0 %all_to_all.74 = bf16[32,256,512]{1,0,2:T(8,128)(2,1)} all-to-all(bf16[32,256,512]{1,0,2:T(8,128)(2,1)} %copy.41), channel_id=1, replica_groups=mesh['seq'=16,'chan'=2] {'chan'}, dimensions={2} | all-to-all | bytes 16777216 | tf_op jit(solution)/shard_map/all_to_all | solution.py:39
  935.7 7.0 all-to-all-start.2
  942.7 16.7 %copy.60 = bf16[32,256,2,256]{1,2,3,0:T(2,128)(2,1)} copy(bf16[32,256,2,256]{1,0,3,2:T(8,128)(2,1)} %bitcast.41) | data formatting | bytes 16777216 | tf_op jit(solution)/shard_map/all_to_all | solution.py:39
  959.4 14.1 %all_to_all.67 = bf16[32,512,256]{1,2,0:T(8,128)(2,1)} reshape(bf16[32,2,256,256]{2,1,3,0:T(2,128)(2,1)} %bitcast.44) | data formatting | bytes 16777216 | tf_op jit(solution)/shard_map/all_to_all | solution.py:39
  973.5 11.5 copy.44
  985.0 119.1 %all-to-all-done.2 = bf16[512,256,32]{1,2,0:T(8,128)(2,1)} async-done(((bf16[512,256,32]{1,2,0:T(8,128)(2,1)}), bf16[512,256,32]{1,2,0:T(8,128)(2,1)}, u32[]{:S(2)}, u32[]{:S(2)}) %all-to-all-start.2) | async-done | bytes 8388640 | tf_op jit(solution)/shard_map/all_to_all | solution.py:45
  1104.2 16.5 %copy.40 = bf16[256,2,256,32]{2,1,0,3:T(2,128)(2,1)} copy(bf16[256,2,256,32]{2,3,0,1:T(8,128)(2,1)} %bitcast.14) | data formatting | bytes 16777216 | tf_op jit(solution)/shard_map/all_to_all | solution.py:45
  1120.7 14.1 %all_to_all.63 = bf16[256,512,32]{1,0,2:T(8,128)(2,1)} reshape(bf16[256,2,256,32]{2,1,0,3:T(2,128)(2,1)} %copy.40) | data formatting | bytes 16777216 | tf_op jit(solution)/shard_map/all_to_all | solution.py:45
  1134.7 15.6 %fusion.1 = bf16[32,256,512]{2,1,0:T(8,128)(2,1)} fusion(bf16[32,256,512]{2,1,0:T(8,128)(2,1)} %param.9, bf16[32,256,512]{1,2,0:T(8,128)(2,1)} %bitcast.38, bf16[32,512,512]{2,1,0:T(8,128)(2,1)} %all-gather.5.cloned.1.call-done), kind=kOutput, calls=%fused_computation.6 | convolution fusion | flops 4320133120 | bytes 41943040 | tf_op jit(solution)/shard_map/coi,cdi->cdo/dot_general | solution.py:29
  1150.4 14.1 %multiply_convert_fusion.2 = bf16[32,256,512]{2,1,0:T(8,128)(2,1)} fusion(bf16[256,512,32]{1,0,2:T(8,128)(2,1)} %all_to_all.63, bf16[512,32,512]{2,0,1:T(8,128)(2,1)} %all-gather.9.cloned.1.call-done), kind=kOutput, calls=%fused_computation.11 | convolution fusion | flops 4303355904 | bytes 33554432 | tf_op jit(solution)/shard_map/odr,dri->roi/dot_general | solution.py:47
  1164.4 13.8 %multiply_convert_fusion.1 = bf16[32,256,512]{2,1,0:T(8,128)(2,1)} fusion(bf16[32,512,256]{1,2,0:T(8,128)(2,1)} %all_to_all.67, bf16[32,512,512]{2,1,0:T(8,128)(2,1)} %all-gather.11.cloned.1.call-done), kind=kOutput, calls=%fused_computation.10 | convolution fusion | flops 4303355904 | bytes 33554432 | tf_op jit(solution)/shard_map/cdo,cdi->coi/dot_general | solution.py:41
  (4 shorter events, 0.0 us)
Async XLA Ops:
  7.2 204.0 %all-gather.5.cloned.1.call-start = ((), (), s32[]{:S(2)}) async-start(), calls=%async_computation.4 | async-start | bytes 25165824 | tf_op jit(solution)/shard_map/all_gather | solution.py:20
  7.9 434.2 %all-gather.7.cloned.1.call-start = ((), (), s32[]{:S(2)}) async-start(), calls=%async_computation.5 | async-start | bytes 25165824 | tf_op jit(solution)/shard_map/all_gather | solution.py:19
  8.6 1141.7 %all-gather.9.cloned.1.call-start = ((), (), s32[]{:S(2)}) async-start(), calls=%async_computation.6 | async-start | bytes 25165824 | tf_op jit(solution)/shard_map/all_gather | solution.py:17
  486.3 678.1 %all-gather.11.cloned.1.call-start = ((), (), s32[]{:S(2)}) async-start(), calls=%async_computation.7 | async-start | bytes 25165824 | tf_op jit(solution)/shard_map/all_gather | solution.py:27
  935.7 168.5 %all-to-all-start.2 = ((bf16[512,256,32]{1,2,0:T(8,128)(2,1)}), bf16[512,256,32]{1,2,0:T(8,128)(2,1)}, u32[]{:S(2)}, u32[]{:S(2)}) async-start(bf16[512,256,32]{1,2,0:T(8,128)(2,1)} %bitcast.40), calls=%async_computation.2 | async-start | bytes 16777216 | tf_op jit(solution)/shard_map/all_to_all | solution.py:45
Sparse Core Ops, SparseCore 0:
  9.5 201.5 all-gather.4
  212.7 198.8 all-gather.6
  486.4 198.9 all-gather.8
  725.6 357.3 all-gather.10
where the time goes:
time: 1190 us
  blocking collectives  571 us (48%)
  waiting for transfers between devices  313 us (26%)
  local copies, waits for them, and re-layouts  151 us (13%)
  matrix products  101 us (8%)
  other arithmetic  28 us (2%)
  between operations  14 us (1%)
    all_to_all x1, blocking collectives, shards(): lax.all_to_all(grad_second, 'chan', split_axis=2, concat_axis=1, tiled=True)  195 us
    all_gather x1, waiting for transfers between devices, shards(): lax.all_gather(second_mixing_blocks, 'chan', axis=1, tiled=True)  193 us
    all_to_all x1, blocking collectives, shards(): lax.all_to_all(grad_first_cols, 'seq', split_axis=2, concat_axis=0, tiled...  188 us
    all_to_all x1, blocking collectives, shards(): lax.all_to_all(first, 'seq', split_axis=0, concat_axis=2, tiled=True)  188 us
    all_to_all x1, waiting for transfers between devices, shards(): lax.all_to_all(grad_first, 'chan', split_axis=0, concat_axis=1, tiled=True)  119 us
    all_to_all x2, local copies, waits for them, and re-layouts, shards(): lax.all_to_all(grad_second, 'chan', split_axis=2, concat_axis=1, tiled=True)  30.8 us
    all_to_all x2, local copies, waits for them, and re-layouts, shards(): lax.all_to_all(grad_first, 'chan', split_axis=0, concat_axis=1, tiled=True)  30.6 us
    dot_general x1, matrix products, shards(): jnp.einsum('rgoi,godr->gdri', group_weight, group_grad, preferred_element...  26.1 us
  transfers between devices with their start and end apart: 5, of which 2 were waited for; matrix products, arithmetic and copies ran while one was open for 16% of the time, Pallas kernels for 0%

commit v1 on v0

v1 whole, which is shorter than its diff:
```python
import math

import jax
import jax.numpy as jnp
from jax import lax
from jax.sharding import PartitionSpec as P


CHUNKS = 4


def f32(x):
    return x.astype(jnp.float32)


def bf16(x):
    return x.astype(jnp.bfloat16)


def dot(spec, a, b):
    return jnp.einsum(spec, a, b, preferred_element_type=jnp.float32)


def gather_half(own):
    count = lax.axis_size("chan")
    if count != 2:
        return lax.all_gather(own, "chan", axis=1, tiled=True)
    own, me = lax.optimization_barrier((own, lax.axis_index("chan")))
    first_of_two = me == 0
    other = lax.ppermute(own, "chan", [(0, 1), (1, 0)])
    return jnp.concatenate(
        [jnp.where(first_of_two, own, other), jnp.where(first_of_two, other, own)], axis=1
    )


def reduce_ring(partial_of):
    count = lax.axis_size("chan")
    me = lax.axis_index("chan")
    ring = [(k, (k + 1) % count) for k in range(count)]
    total = None
    for step in range(count):
        block = lax.rem(me + (2 * count - 1 - step), count)
        part = partial_of(block)
        total = part if total is None else part + f32(total)
        if step < count - 1:
            total = bf16(total)
            total = lax.ppermute(total, "chan", ring)
    return bf16(total)


def shards(inputs, gate_in, gate_out, cotangent, mix_one, second_mixing_blocks):
    count = lax.axis_size("chan")
    seq = lax.axis_size("seq")
    one_scale = 1.0 / math.sqrt(mix_one.shape[2])
    two_scale = 1.0 / math.sqrt(second_mixing_blocks.shape[2])
    rows = mix_one.shape[0]
    cols = second_mixing_blocks.shape[0]
    chans = inputs.shape[0]
    chunks = math.gcd(CHUNKS, rows)

    weights_one = [gather_half(w) for w in jnp.split(mix_one, chunks, axis=0)]
    weights_two = [gather_half(w) for w in jnp.split(second_mixing_blocks, chunks, axis=0)]
    gated = bf16(f32(inputs) * f32(gate_in))
    grad_second = bf16(f32(cotangent) * f32(gate_out))

    parts = []
    for w, x in zip(weights_one, jnp.split(gated, chunks, axis=1)):
        first = bf16(dot("roi,dri->odr", w, x) * one_scale)
        first = first.reshape(seq, cols, chans, first.shape[2])
        got = lax.all_to_all(first, "seq", split_axis=0, concat_axis=0)
        parts.append(got)
    first_cols = jnp.stack(parts, axis=0)
    first_cols = jnp.transpose(first_cols, (2, 3, 1, 0, 4)).reshape(cols, chans, seq * rows)

    backs = []
    for w, g in zip(weights_two, jnp.split(grad_second, chunks, axis=0)):
        back = bf16(dot("coi,cdo->icd", w, g) * two_scale)
        back = back.reshape(seq, rows, back.shape[1], chans)
        got = lax.all_to_all(back, "seq", split_axis=0, concat_axis=0)
        backs.append(got)
    grad_first = jnp.stack(backs, axis=0)
    grad_first = jnp.transpose(grad_first, (2, 1, 0, 3, 4)).reshape(rows, seq * cols, chans)

    half_two = grad_second.shape[2] // count
    half_one = (seq * cols) // count

    def part_two(block):
        g = lax.dynamic_slice_in_dim(grad_second, block * half_two, half_two, axis=2)
        return dot("cdo,cdi->coi", g, first_cols) * two_scale

    def part_one(block):
        g = lax.dynamic_slice_in_dim(grad_first, block * half_one, half_one, axis=1)
        return dot("rod,dri->roi", g, gated) * one_scale

    grad_mix_two = reduce_ring(part_two)
    grad_mix_one = reduce_ring(part_one)

    full_two = jnp.concatenate(weights_two, axis=0)
    full_one = jnp.concatenate(weights_one, axis=0)
    second = bf16(dot("coi,cdi->cdo", full_two, first_cols) * two_scale)
    grad_gate_out = bf16(f32(cotangent) * f32(second))
    grad_gated = bf16(dot("roi,rod->dri", full_one, grad_first) * one_scale)
    grad_input = bf16(f32(grad_gated) * f32(gate_in))
    return (grad_input, grad_gate_out, grad_mix_one, grad_mix_two)


def solution(mesh):
    rows_first = P("seq", "chan", None)
    chan_first = P("chan", "seq", None)
    return jax.shard_map(
        shards,
        mesh=mesh,
        in_specs=(chan_first, chan_first, rows_first, rows_first, rows_first, rows_first),
        out_specs=(chan_first, rows_first, rows_first, rows_first),
        check_vma=False,
    )
```

time: 1190 us -> 890 us (0.75)
  blocking collectives: 571 us -> 0 us
  waiting for transfers between devices: 313 us -> 470 us
  starting transfers between devices: 7.15 us -> 99.8 us
  matrix products: 101 us -> 161 us
  local copies, waits for them, and re-layouts: 151 us -> 91 us
  other arithmetic: 28 us -> 55.1 us
  between operations: 14 us -> 1.17 us
    all_to_all x3 -> x0, blocking collectives: 571 us -> none  [the longest x1 195 us: shards(): lax.all_to_all(grad_second, 'chan', split_axis=2, concat_axis=1, tiled=True)]
    ppermute x0 -> x10, waiting for transfers between devices: none -> 333 us  [the longest x2 236 us: reduce_ring(): total = lax.ppermute(total, 'chan', ring)]
    all_gather x4 -> x0, waiting for transfers between devices: 193 us -> none  [the longest x1 193 us: shards(): lax.all_gather(second_mixing_blocks, 'chan', axis=1, tiled=True)]
    all_to_all x7 -> x0, local copies, waits for them, and re-layouts: 93.8 us -> none  [the longest x2 30.8 us: shards(): lax.all_to_all(grad_second, 'chan', split_axis=2, concat_axis=1, tiled=True)]
    all_to_all x1 -> x8, starting transfers between devices: 7 us -> 85.4 us  [the longest x4 45.5 us: shards(): got = lax.all_to_all(first, 'seq', split_axis=0, concat_axis=0)]
    dot_general x6 -> x14, matrix products: 101 us -> 161 us  [dot(): return jnp.einsum(spec, a, b, preferred_element_type=jnp.float32)]
    select_n x0 -> x8, other arithmetic: none -> 22.5 us  [gather_half(): jnp.where(first_of_two, own, other)]
    all_to_all x1 -> x8, waiting for transfers between devices: 119 us -> 137 us  [the longest x4 106 us: shards(): got = lax.all_to_all(first, 'seq', split_axis=0, concat_axis=0)]
  transfers between devices with their start and end apart: 5 -> 18, of which waited for: 2 -> 13; matrix products, arithmetic and copies ran while one was open for 16% -> 28% of each run, Pallas kernels for 0% -> 0%
where the time goes in v1:
time: 890 us; the launch traced here: 878 us
  waiting for transfers between devices  470 us (53%)
  matrix products  161 us (18%)
  starting transfers between devices  99.8 us (11%)
  local copies, waits for them, and re-layouts  91 us (10%)
  other arithmetic  55.1 us (6%)
    ppermute x2, waiting for transfers between devices, reduce_ring(): total = lax.ppermute(total, 'chan', ring)  236 us
    dot_general x14, matrix products, dot(): return jnp.einsum(spec, a, b, preferred_element_type=jnp.float32)  161 us
    all_to_all x4, waiting for transfers between devices, shards(): got = lax.all_to_all(first, 'seq', split_axis=0, concat_axis=0)  106 us
    ppermute x8, waiting for transfers between devices, gather_half(): other = lax.ppermute(own, 'chan', [(0, 1), (1, 0)])  96.8 us
    all_to_all x4, starting transfers between devices, shards(): got = lax.all_to_all(first, 'seq', split_axis=0, concat_axis=0)  45.5 us
    all_to_all x4, starting transfers between devices, shards(): got = lax.all_to_all(back, 'seq', split_axis=0, concat_axis=0)  40 us
    convert_element_type x8, local copies, waits for them, and re-layouts, bf16(): return x.astype(jnp.bfloat16)  34.6 us
    all_to_all x4, waiting for transfers between devices, shards(): got = lax.all_to_all(back, 'seq', split_axis=0, concat_axis=0)  31 us
  transfers between devices with their start and end apart: 18, of which 13 were waited for; matrix products, arithmetic and copies ran while one was open for 28% of the time, Pallas kernels for 0%

profile of v1, /device:TPU:0, one launch (start us, length us, event | category | flops | bytes accessed | tf_op | source)
XLA Modules:
  0.0 878.4 jit_solution(4285249385045650527)
XLA Ops:
  9.4 7.2 fusion
  16.6 39.3 %collective-permute-done.3 = bf16[8,256,512]{2,1,0:T(8,128)(2,1)} collective-permute-done((bf16[8,256,512]{2,1,0:T(8,128)(2,1)S(1)}, bf16[8,256,512]{2,1,0:T(8,128)(2,1)}, u32[]{:S(2)}, u32[]{:S(2)}) %collective-permute-start.3) | collective-permute-done | bytes 2097184 | tf_op jit(solution)/shard_map/ppermute | solution.py:30
  72.3 28.5 %collective-permute-done.2 = bf16[8,256,512]{2,1,0:T(8,128)(2,1)} collective-permute-done((bf16[8,256,512]{2,1,0:T(8,128)(2,1)}, bf16[8,256,512]{2,1,0:T(8,128)(2,1)}, u32[]{:S(2)}, u32[]{:S(2)}) %collective-permute-start.2) | collective-permute-done | bytes 2097184 | tf_op jit(solution)/shard_map/ppermute | solution.py:30
  112.2 10.8 %all-to-all-start.2 = ((bf16[16,32,8,256]{3,2,1,0:T(8,128)(2,1)}), bf16[16,32,8,256]{3,2,1,0:T(8,128)(2,1)}, u32[]{:S(2)}, u32[]{:S(2)}) async-start(bf16[16,32,8,256]{3,2,1,0:T(8,128)(2,1)} %bitcast.7), calls=%async_computation.2 | async-start | bytes 4194304 | tf_op jit(solution)/shard_map/all_to_all | solution.py:79
  124.6 21.2 %collective-permute-done.1 = bf16[8,256,512]{2,1,0:T(8,128)(2,1)} collective-permute-done((bf16[8,256,512]{2,1,0:T(8,128)(2,1)}, bf16[8,256,512]{2,1,0:T(8,128)(2,1)}, u32[]{:S(2)}, u32[]{:S(2)}) %collective-permute-start.1) | collective-permute-done | bytes 2097184 | tf_op jit(solution)/shard_map/ppermute | solution.py:30
  164.1 11.3 %all-to-all-start.1 = ((bf16[16,32,8,256]{3,2,1,0:T(8,128)(2,1)}), bf16[16,32,8,256]{3,2,1,0:T(8,128)(2,1)}, u32[]{:S(2)}, u32[]{:S(2)}) async-start(bf16[16,32,8,256]{3,2,1,0:T(8,128)(2,1)} %bitcast.4), calls=%async_computation.1 | async-start | bytes 4194304 | tf_op jit(solution)/shard_map/all_to_all | solution.py:79
  182.8 7.9 collective-permute-done
  203.7 12.6 %all-to-all-done.1 = bf16[16,32,8,256]{3,2,1,0:T(8,128)(2,1)} async-done(((bf16[16,32,8,256]{3,2,1,0:T(8,128)(2,1)}), bf16[16,32,8,256]{3,2,1,0:T(8,128)(2,1)}, u32[]{:S(2)}, u32[]{:S(2)}) %all-to-all-start.1) | async-done | bytes 2097184 | tf_op jit(solution)/shard_map/all_to_all | solution.py:79
  216.4 11.5 %all-to-all-start = ((bf16[16,32,8,256]{3,2,1,0:T(8,128)(2,1)}), bf16[16,32,8,256]{3,2,1,0:T(8,128)(2,1)}, u32[]{:S(2)}, u32[]{:S(2)}) async-start(bf16[16,32,8,256]{3,2,1,0:T(8,128)(2,1)} %bitcast.1), calls=%async_computation | async-start | bytes 4194304 | tf_op jit(solution)/shard_map/all_to_all | solution.py:79
  229.4 11.6 %fusion.3 = bf16[256,32,512]{2,0,1:T(8,128)(2,1)S(1)} fusion(bf16[256,32,512]{2,1,0:T(8,128)(2,1)} %param.6, bf16[256,32,512]{2,1,0:T(8,128)(2,1)} %param.7), kind=kLoop, calls=%fused_computation.7 | loop fusion | flops 16777216 | bytes 25165824 | tf_op jit(solution)/shard_map/convert_element_type | solution.py:17
  255.7 13.1 %all-to-all-done = bf16[16,32,8,256]{3,2,1,0:T(8,128)(2,1)} async-done(((bf16[16,32,8,256]{3,2,1,0:T(8,128)(2,1)}), bf16[16,32,8,256]{3,2,1,0:T(8,128)(2,1)}, u32[]{:S(2)}, u32[]{:S(2)}) %all-to-all-start) | async-done | bytes 2097184 | tf_op jit(solution)/shard_map/all_to_all | solution.py:79
  268.8 11.3 %all-to-all-start.7 = ((bf16[16,32,256,8]{2,3,1,0:T(8,128)(2,1)}), bf16[16,32,256,8]{2,3,1,0:T(8,128)(2,1)}, u32[]{:S(2)}, u32[]{:S(2)}) async-start(bf16[16,32,256,8]{2,3,1,0:T(8,128)(2,1)} %bitcast.25), calls=%async_computation.7 | async-start | bytes 4194304 | tf_op jit(solution)/shard_map/all_to_all | solution.py:70
  295.0 26.2 %all-to-all-done.7 = bf16[16,32,256,8]{2,3,1,0:T(8,128)(2,1)} async-done(((bf16[16,32,256,8]{2,3,1,0:T(8,128)(2,1)}), bf16[16,32,256,8]{2,3,1,0:T(8,128)(2,1)}, u32[]{:S(2)}, u32[]{:S(2)}) %all-to-all-start.7) | async-done | bytes 2097184 | tf_op jit(solution)/shard_map/all_to_all | solution.py:70
  321.1 11.3 %all-to-all-start.6 = ((bf16[16,32,256,8]{2,3,1,0:T(8,128)(2,1)}), bf16[16,32,256,8]{2,3,1,0:T(8,128)(2,1)}, u32[]{:S(2)}, u32[]{:S(2)}) async-start(bf16[16,32,256,8]{2,3,1,0:T(8,128)(2,1)} %bitcast.22), calls=%async_computation.6 | async-start | bytes 4194304 | tf_op jit(solution)/shard_map/all_to_all | solution.py:70
  347.3 26.1 %all-to-all-done.6 = bf16[16,32,256,8]{2,3,1,0:T(8,128)(2,1)} async-done(((bf16[16,32,256,8]{2,3,1,0:T(8,128)(2,1)}), bf16[16,32,256,8]{2,3,1,0:T(8,128)(2,1)}, u32[]{:S(2)}, u32[]{:S(2)}) %all-to-all-start.6) | async-done | bytes 2097184 | tf_op jit(solution)/shard_map/all_to_all | solution.py:70
  373.4 11.3 %all-to-all-start.5 = ((bf16[16,32,256,8]{2,3,1,0:T(8,128)(2,1)}), bf16[16,32,256,8]{2,3,1,0:T(8,128)(2,1)}, u32[]{:S(2)}, u32[]{:S(2)}) async-start(bf16[16,32,256,8]{2,3,1,0:T(8,128)(2,1)} %bitcast.19), calls=%async_computation.5 | async-start | bytes 4194304 | tf_op jit(solution)/shard_map/all_to_all | solution.py:70
  398.0 27.7 %all-to-all-done.5 = bf16[16,32,256,8]{2,3,1,0:T(8,128)(2,1)} async-done(((bf16[16,32,256,8]{2,3,1,0:T(8,128)(2,1)}), bf16[16,32,256,8]{2,3,1,0:T(8,128)(2,1)}, u32[]{:S(2)}, u32[]{:S(2)}) %all-to-all-start.5) | async-done | bytes 2097184 | tf_op jit(solution)/shard_map/all_to_all | solution.py:70
  425.7 11.7 %all-to-all-start.4 = ((bf16[16,32,256,8]{2,3,1,0:T(8,128)(2,1)}), bf16[16,32,256,8]{2,3,1,0:T(8,128)(2,1)}, u32[]{:S(2)}, u32[]{:S(2)}) async-start(bf16[16,32,256,8]{2,3,1,0:T(8,128)(2,1)} %bitcast.16), calls=%async_computation.4 | async-start | bytes 4194304 | tf_op jit(solution)/shard_map/all_to_all | solution.py:70
  437.4 6.6 maximum_bitcast_fusion
  444.1 7.9 copy.23
  452.0 26.5 %all-to-all-done.4 = bf16[16,32,256,8]{2,3,1,0:T(8,128)(2,1)} async-done(((bf16[16,32,256,8]{2,3,1,0:T(8,128)(2,1)}), bf16[16,32,256,8]{2,3,1,0:T(8,128)(2,1)}, u32[]{:S(2)}, u32[]{:S(2)}) %all-to-all-start.4) | async-done | bytes 2097184 | tf_op jit(solution)/shard_map/all_to_all | solution.py:70
  478.4 7.2 maximum_bitcast_fusion.1
  485.6 7.8 copy.31
  493.4 10.4 %multiply_convert_fusion.1 = bf16[32,256,512]{2,1,0:T(8,128)(2,1)} fusion(bf16[256,32,512]{2,0,1:T(8,128)(2,1)} %copy-done, bf16[32,512,256]{2,1,0:T(8,128)(2,1)} %bitcast.60, s32[]{:T(128)S(6)} %select_n.115), kind=kOutput, calls=%fused_computation.43 | convolution fusion | flops 2155872256 | bytes 20971524 | tf_op jit(solution)/shard_map/rod,dri->roi/dot_general | solution.py:21
  505.4 8.6 multiply_convert_fusion
  514.5 52.5 %fusion.2 = bf16[256,32,512]{2,0,1:T(8,128)(2,1)} fusion(bf16[256,32,512]{2,1,0:T(8,128)(2,1)} %param.7, bf16[32,512,256]{2,1,0:T(8,128)(2,1)} %bitcast.61, bf16[8,256,512]{2,1,0:T(8,128)(2,1)S(1)} %copy-done.16, bf16[8,256,512]{2,1,0:T(8,128)(2,1)S(1)} %copy-done.14, bf16[8,256,512]{2,1,0:T(8,128)(2,1)} %copy-done.19, ...), kind=kOutput, calls=%fused_computation.6 | convolution fusion | flops 4454350848 | bytes 41943040 | tf_op jit(solution)/shard_map/roi,rod->dri/dot_general | solution.py:21
  567.0 11.7 %copy.37 = bf16[256,32,512]{2,1,0:T(8,128)(2,1)} copy(bf16[256,32,512]{2,0,1:T(8,128)(2,1)} %fusion.2) | data formatting | bytes 16777216
  578.6 39.7 %fusion.1 = bf16[32,256,512]{2,1,0:T(8,128)(2,1)} fusion(bf16[32,256,512]{2,1,0:T(8,128)(2,1)} %param.9, bf16[32,256,512]{1,2,0:T(8,128)(2,1)} %bitcast.58, bf16[8,256,512]{2,1,0:T(8,128)(2,1)} %copy-done.6, bf16[8,256,512]{2,1,0:T(8,128)(2,1)S(1)} %copy-done.5, bf16[8,256,512]{2,1,0:T(8,128)(2,1)} %copy-done.8, bf16[8,256,512]{2,1,0:T(8,128)(2,1)} %copy-done.7, ...), kind=kOutput, calls=%fused_computation.5 | convolution fusion | flops 4454350848 | bytes 41943040 | tf_op jit(solution)/shard_map/coi,cdi->cdo/dot_general | solution.py:21
  618.4 69.1 %collective-permute-done.8 = bf16[32,256,512]{2,1,0:T(8,128)(2,1)} collective-permute-done((bf16[32,256,512]{2,1,0:T(8,128)(2,1)}, bf16[32,256,512]{2,1,0:T(8,128)(2,1)}, u32[]{:S(2)}, u32[]{:S(2)}) %collective-permute-start.8) | collective-permute-done | bytes 8388640 | tf_op jit(solution)/shard_map/ppermute | solution.py:47
  687.5 12.8 %add_convert_fusion.1 = bf16[32,256,512]{2,1,0:T(8,128)(2,1)} fusion(bf16[32,256,512]{2,1,0:T(8,128)(2,1)} %collective-permute-done.8, bf16[256,32,512]{2,0,1:T(8,128)(2,1)} %copy-done, bf16[32,512,256]{2,1,0:T(8,128)(2,1)} %bitcast.62, s32[]{:T(128)S(6)} %select_n.114), kind=kOutput, calls=%fused_computation.42 | convolution fusion | flops 2164260864 | bytes 29360132 | tf_op jit(solution)/shard_map/rod,dri->roi/dot_general | solution.py:21
  700.3 167.0 %collective-permute-done.9 = bf16[32,256,512]{2,1,0:T(8,128)(2,1)} collective-permute-done((bf16[32,256,512]{2,1,0:T(8,128)(2,1)}, bf16[32,256,512]{2,1,0:T(8,128)(2,1)}, u32[]{:S(2)}, u32[]{:S(2)}) %collective-permute-start.9) | collective-permute-done | bytes 8388640 | tf_op jit(solution)/shard_map/ppermute | solution.py:47
  867.3 10.9 %add_convert_fusion = bf16[32,256,512]{2,1,0:T(8,128)(2,1)} fusion(bf16[32,256,512]{2,1,0:T(8,128)(2,1)} %collective-permute-done.9, bf16[32,256,512]{1,2,0:T(8,128)(2,1)} %bitcast.59, bf16[32,256,512]{2,1,0:T(8,128)(2,1)} %copy-done.2, s32[]{:T(128)S(6)} %select_n.114), kind=kOutput, calls=%fused_computation.40 | convolution fusion | flops 2164260864 | bytes 29360132 | tf_op jit(solution)/shard_map/cdo,cdi->coi/dot_general | solution.py:21
  (91 shorter events, 138.2 us)
Async XLA Ops:
  6.3 49.5 %collective-permute-start.3 = (bf16[8,256,512]{2,1,0:T(8,128)(2,1)S(1)}, bf16[8,256,512]{2,1,0:T(8,128)(2,1)}, u32[]{:S(2)}, u32[]{:S(2)}) collective-permute-start(bf16[8,256,512]{2,1,0:T(8,128)(2,1)S(1)} %get-tuple-element.27), channel_id=1, source_target_pairs={{0,1},{1,0},{2,3},{3,2},{4,5},{5,4},{6,7},{7,6},{8,9},{9,8},{10,11... | collective-permute-start | bytes 6291464 | tf_op jit(solution)/shard_map/ppermute | solution.py:30
  9.3 91.5 %collective-permute-start.2 = (bf16[8,256,512]{2,1,0:T(8,128)(2,1)}, bf16[8,256,512]{2,1,0:T(8,128)(2,1)}, u32[]{:S(2)}, u32[]{:S(2)}) collective-permute-start(bf16[8,256,512]{2,1,0:T(8,128)(2,1)} %get-tuple-element.25), channel_id=1, source_target_pairs={{0,1},{1,0},{2,3},{3,2},{4,5},{5,4},{6,7},{7,6},{8,9},{9,8},{10,11... | collective-permute-start | bytes 6291464 | tf_op jit(solution)/shard_map/ppermute | solution.py:30
  16.5 41.2 %copy-start.2 = (bf16[32,256,512]{2,1,0:T(8,128)(2,1)}, bf16[32,256,512]{2,1,0:T(8,128)(2,1)S(1)}, u32[]{:S(2)}) copy-start(bf16[32,256,512]{2,1,0:T(8,128)(2,1)S(1)} %fusion) | copy-start | bytes 25165828
  57.8 2.0 copy-start.6
  64.3 47.9 %all-to-all-start.3 = ((bf16[16,32,8,256]{3,2,1,0:T(8,128)(2,1)}), bf16[16,32,8,256]{3,2,1,0:T(8,128)(2,1)S(1)}, u32[]{:S(2)}, u32[]{:S(2)}) async-start(bf16[16,32,8,256]{3,2,1,0:T(8,128)(2,1)} %bitcast.10), calls=%async_computation.3 | async-start | bytes 4194304 | tf_op jit(solution)/shard_map/all_to_all | solution.py:79
  70.8 75.0 %collective-permute-start.1 = (bf16[8,256,512]{2,1,0:T(8,128)(2,1)}, bf16[8,256,512]{2,1,0:T(8,128)(2,1)}, u32[]{:S(2)}, u32[]{:S(2)}) collective-permute-start(bf16[8,256,512]{2,1,0:T(8,128)(2,1)} %get-tuple-element.23), channel_id=1, source_target_pairs={{0,1},{1,0},{2,3},{3,2},{4,5},{5,4},{6,7},{7,6},{8,9},{9,8},{10,11... | collective-permute-start | bytes 6291464 | tf_op jit(solution)/shard_map/ppermute | solution.py:30
  72.3 32.9 %copy-start.3 = (bf16[32,256,512]{2,1,0:T(8,128)(2,1)S(1)}, bf16[32,256,512]{2,1,0:T(8,128)(2,1)}, u32[]{:S(2)}) copy-start(bf16[32,256,512]{2,1,0:T(8,128)(2,1)} %copy-done.2) | copy-start | bytes 25165828
  112.2 51.8 %all-to-all-start.2 = ((bf16[16,32,8,256]{3,2,1,0:T(8,128)(2,1)}), bf16[16,32,8,256]{3,2,1,0:T(8,128)(2,1)}, u32[]{:S(2)}, u32[]{:S(2)}) async-start(bf16[16,32,8,256]{3,2,1,0:T(8,128)(2,1)} %bitcast.7), calls=%async_computation.2 | async-start | bytes 4194304 | tf_op jit(solution)/shard_map/all_to_all | solution.py:79
  123.0 67.7 %collective-permute-start = (bf16[8,256,512]{2,1,0:T(8,128)(2,1)}, bf16[8,256,512]{2,1,0:T(8,128)(2,1)}, u32[]{:S(2)}, u32[]{:S(2)}) collective-permute-start(bf16[8,256,512]{2,1,0:T(8,128)(2,1)} %get-tuple-element.21), channel_id=1, source_target_pairs={{0,1},{1,0},{2,3},{3,2},{4,5},{5,4},{6,7},{7,6},{8,9},{9,8},{10,11... | collective-permute-start | bytes 6291464 | tf_op jit(solution)/shard_map/ppermute | solution.py:30
  148.3 2.0 copy-start.10
  164.1 52.3 %all-to-all-start.1 = ((bf16[16,32,8,256]{3,2,1,0:T(8,128)(2,1)}), bf16[16,32,8,256]{3,2,1,0:T(8,128)(2,1)}, u32[]{:S(2)}, u32[]{:S(2)}) async-start(bf16[16,32,8,256]{3,2,1,0:T(8,128)(2,1)} %bitcast.4), calls=%async_computation.1 | async-start | bytes 4194304 | tf_op jit(solution)/shard_map/all_to_all | solution.py:79
  181.3 59.7 %collective-permute-start.7 = (bf16[8,256,512]{2,1,0:T(8,128)(2,1)}, bf16[8,256,512]{2,1,0:T(8,128)(2,1)}, u32[]{:S(2)}, u32[]{:S(2)}) collective-permute-start(bf16[8,256,512]{2,1,0:T(8,128)(2,1)} %get-tuple-element.35), channel_id=1, source_target_pairs={{0,1},{1,0},{2,3},{3,2},{4,5},{5,4},{6,7},{7,6},{8,9},{9,8},{10,11... | collective-permute-start | bytes 6291464 | tf_op jit(solution)/shard_map/ppermute | solution.py:30
  193.2 2.0 copy-start.12
  216.4 52.5 %all-to-all-start = ((bf16[16,32,8,256]{3,2,1,0:T(8,128)(2,1)}), bf16[16,32,8,256]{3,2,1,0:T(8,128)(2,1)}, u32[]{:S(2)}, u32[]{:S(2)}) async-start(bf16[16,32,8,256]{3,2,1,0:T(8,128)(2,1)} %bitcast.1), calls=%async_computation | async-start | bytes 4194304 | tf_op jit(solution)/shard_map/all_to_all | solution.py:79
  227.8 53.8 %collective-permute-start.6 = (bf16[8,256,512]{2,1,0:T(8,128)(2,1)}, bf16[8,256,512]{2,1,0:T(8,128)(2,1)}, u32[]{:S(2)}, u32[]{:S(2)}) collective-permute-start(bf16[8,256,512]{2,1,0:T(8,128)(2,1)} %get-tuple-element.33), channel_id=1, source_target_pairs={{0,1},{1,0},{2,3},{3,2},{4,5},{5,4},{6,7},{7,6},{8,9},{9,8},{10,11... | collective-permute-start | bytes 6291464 | tf_op jit(solution)/shard_map/ppermute | solution.py:30
  241.0 5.6 copy-start
  246.6 2.0 copy-start.15
  268.8 52.3 %all-to-all-start.7 = ((bf16[16,32,256,8]{2,3,1,0:T(8,128)(2,1)}), bf16[16,32,256,8]{2,3,1,0:T(8,128)(2,1)}, u32[]{:S(2)}, u32[]{:S(2)}) async-start(bf16[16,32,256,8]{2,3,1,0:T(8,128)(2,1)} %bitcast.25), calls=%async_computation.7 | async-start | bytes 4194304 | tf_op jit(solution)/shard_map/all_to_all | solution.py:70
  280.1 53.9 %collective-permute-start.5 = (bf16[8,256,512]{2,1,0:T(8,128)(2,1)}, bf16[8,256,512]{2,1,0:T(8,128)(2,1)}, u32[]{:S(2)}, u32[]{:S(2)}) collective-permute-start(bf16[8,256,512]{2,1,0:T(8,128)(2,1)} %get-tuple-element.31), channel_id=1, source_target_pairs={{0,1},{1,0},{2,3},{3,2},{4,5},{5,4},{6,7},{7,6},{8,9},{9,8},{10,11... | collective-permute-start | bytes 6291464 | tf_op jit(solution)/shard_map/ppermute | solution.py:30
  281.7 6.2 copy-start.1
  284.3 2.1 copy-start.19
  321.1 52.3 %all-to-all-start.6 = ((bf16[16,32,256,8]{2,3,1,0:T(8,128)(2,1)}), bf16[16,32,256,8]{2,3,1,0:T(8,128)(2,1)}, u32[]{:S(2)}, u32[]{:S(2)}) async-start(bf16[16,32,256,8]{2,3,1,0:T(8,128)(2,1)} %bitcast.22), calls=%async_computation.6 | async-start | bytes 4194304 | tf_op jit(solution)/shard_map/all_to_all | solution.py:70
  332.4 52.3 %collective-permute-start.4 = (bf16[8,256,512]{2,1,0:T(8,128)(2,1)}, bf16[8,256,512]{2,1,0:T(8,128)(2,1)}, u32[]{:S(2)}, u32[]{:S(2)}) collective-permute-start(bf16[8,256,512]{2,1,0:T(8,128)(2,1)} %get-tuple-element.29), channel_id=1, source_target_pairs={{0,1},{1,0},{2,3},{3,2},{4,5},{5,4},{6,7},{7,6},{8,9},{9,8},{10,11... | collective-permute-start | bytes 6291464 | tf_op jit(solution)/shard_map/ppermute | solution.py:30
  373.4 52.3 %all-to-all-start.5 = ((bf16[16,32,256,8]{2,3,1,0:T(8,128)(2,1)}), bf16[16,32,256,8]{2,3,1,0:T(8,128)(2,1)}, u32[]{:S(2)}, u32[]{:S(2)}) async-start(bf16[16,32,256,8]{2,3,1,0:T(8,128)(2,1)} %bitcast.19), calls=%async_computation.5 | async-start | bytes 4194304 | tf_op jit(solution)/shard_map/all_to_all | solution.py:70
  387.2 2.0 copy-start.23
  425.7 52.7 %all-to-all-start.4 = ((bf16[16,32,256,8]{2,3,1,0:T(8,128)(2,1)}), bf16[16,32,256,8]{2,3,1,0:T(8,128)(2,1)}, u32[]{:S(2)}, u32[]{:S(2)}) async-start(bf16[16,32,256,8]{2,3,1,0:T(8,128)(2,1)} %bitcast.16), calls=%async_computation.4 | async-start | bytes 4194304 | tf_op jit(solution)/shard_map/all_to_all | solution.py:70
  503.9 183.6 %collective-permute-start.8 = (bf16[32,256,512]{2,1,0:T(8,128)(2,1)}, bf16[32,256,512]{2,1,0:T(8,128)(2,1)}, u32[]{:S(2)}, u32[]{:S(2)}) collective-permute-start(bf16[32,256,512]{2,1,0:T(8,128)(2,1)} %multiply_convert_fusion.1), channel_id=1, source_target_pairs={{0,1},{1,0},{2,3},{3,2},{4,5},{5,4},{6,7},{7,6},{8,9},{9,8},{10,11... | collective-permute-start | bytes 25165832 | tf_op jit(solution)/shard_map/ppermute | solution.py:47
  505.4 9.2 %copy-start.14 = (bf16[8,256,512]{2,1,0:T(8,128)(2,1)S(1)}, bf16[8,256,512]{2,1,0:T(8,128)(2,1)}, u32[]{:S(2)}) copy-start(bf16[8,256,512]{2,1,0:T(8,128)(2,1)} %copy-done.13) | copy-start | bytes 6291460
  505.4 9.2 %copy-start.16 = (bf16[8,256,512]{2,1,0:T(8,128)(2,1)S(1)}, bf16[8,256,512]{2,1,0:T(8,128)(2,1)}, u32[]{:S(2)}) copy-start(bf16[8,256,512]{2,1,0:T(8,128)(2,1)} %copy-done.15) | copy-start | bytes 6291460
  505.4 9.2 %copy-start.18 = (bf16[8,256,512]{2,1,0:T(8,128)(2,1)S(1)}, bf16[8,256,512]{2,1,0:T(8,128)(2,1)}, u32[]{:S(2)}) copy-start(bf16[8,256,512]{2,1,0:T(8,128)(2,1)} %copy-done.17) | copy-start | bytes 6291460
  514.0 353.3 %collective-permute-start.9 = (bf16[32,256,512]{2,1,0:T(8,128)(2,1)}, bf16[32,256,512]{2,1,0:T(8,128)(2,1)}, u32[]{:S(2)}, u32[]{:S(2)}) collective-permute-start(bf16[32,256,512]{2,1,0:T(8,128)(2,1)} %multiply_convert_fusion), channel_id=1, source_target_pairs={{0,1},{1,0},{2,3},{3,2},{4,5},{5,4},{6,7},{7,6},{8,9},{9,8},{10,11... | collective-permute-start | bytes 25165832 | tf_op jit(solution)/shard_map/ppermute | solution.py:47
  567.0 11.7 %copy-start.5 = (bf16[8,256,512]{2,1,0:T(8,128)(2,1)S(1)}, bf16[8,256,512]{2,1,0:T(8,128)(2,1)}, u32[]{:S(2)}) copy-start(bf16[8,256,512]{2,1,0:T(8,128)(2,1)} %copy-done.4) | copy-start | bytes 6291460
  (10 other events, 14.7 us)
